TPU v7x, 32 devices: a whole 2x2x4 slice. The times are simulated.
32 devices in a mesh: grp: 2 (over x), sp: 16 (over z, y, core).
Axes of the slice: x: 2, y: 2, z: 4, core: 2. Of those that a mesh axis runs over, the one named last changes fastest.
Arguments:
- volume: bfloat16 [64, 32, 48, 256], P(('grp', 'sp')), parts along dimension 0, may hold values from -8 to 8
- norm_gain: float32 [256], replicated, may hold values from 0.5 to 1.5
- norm_bias: float32 [256], replicated, may hold values from -3 to 3
- conv_weight: bfloat16 [27, 256, 256], replicated, may hold values from -0.078125 to 0.078125
- down_weight: bfloat16 [8, 256, 512], replicated, may hold values from -0.125 to 0.125
Outputs:
- reduced: bfloat16 [32, 16, 24, 512], P(('grp', 'sp')), parts along dimension 0
There are 2 independent parts, one for each index of `grp`. A program takes and returns all parts, laid end to end along the dimension named above; an argument that names none is the same for every part. Nothing has to cross between parts.
All inputs are finite; a program needn't handle non-finite values.
Results may differ from a plain program's by a relative error of at most 0.0058.
Values may be sent and summed in bfloat16 or wider, within the bound.
A program may use at most 192 MiB of HBM per device.

v0:
```python
import jax
import jax.numpy as jnp
from jax import lax
from jax.sharding import PartitionSpec as P

GROUPS = 32


def padded_2(block, sides, width):
    for axis, dim in sides:
        count = lax.axis_size(axis)
        forward = [(i, i + 1) for i in range(count - 1)]
        backward = [(target, source) for source, target in forward]
        low = lax.ppermute(
            lax.slice_in_dim(block, block.shape[dim] - width, None, axis=dim), axis, forward
        )
        high = lax.ppermute(lax.slice_in_dim(block, 0, width, axis=dim), axis, backward)
        block = jnp.concatenate([low, block, high], axis=dim)
    return block


def conv_block(padded, plane_count, row_count, col_count, filters):
    total = None
    for tap_index in range(27):
        shift_d = tap_index // 9
        shift_h = tap_index // 3 % 3
        shift_w = tap_index % 3
        window = padded[
            shift_d : shift_d + plane_count,
            shift_h : shift_h + row_count,
            shift_w : shift_w + col_count,
            :,
        ]
        term = jnp.einsum(
            "dhwc,ck->dhwk", window, filters[tap_index], preferred_element_type=jnp.float32
        )
        total = term if total is None else total + term
    return total


def down_block(hidden, filters):
    total = None
    for tap_index in range(8):
        shift_d = tap_index // 4
        shift_h = tap_index // 2 % 2
        shift_w = tap_index % 2
        window = hidden[shift_d::2, shift_h::2, shift_w::2, :]
        term = jnp.einsum(
            "dhwc,ck->dhwk", window, filters[tap_index], preferred_element_type=jnp.float32
        )
        total = term if total is None else total + term
    return total


def body(volume, norm_gain, norm_bias, conv_weight, down_weight):
    plane_count, row_count, col_count, channels = volume.shape
    per_group = channels // GROUPS
    source = volume.astype(jnp.float32)
    grouped = source.reshape(plane_count, row_count, col_count, GROUPS, per_group)
    local_total = jnp.sum(grouped, axis=(0, 1, 2, 4))
    local_squares = jnp.sum(grouped * grouped, axis=(0, 1, 2, 4))
    total, squares = lax.psum((local_total, local_squares), "sp")
    count = plane_count * lax.axis_size("sp") * row_count * col_count * per_group
    mean = total / count
    var = squares / count - mean * mean
    inv = 1.0 / jnp.sqrt(var + 1e-05)
    scale = norm_gain * jnp.repeat(inv, per_group)
    shift = norm_bias - jnp.repeat(mean, per_group) * scale
    normed = (source * scale + shift).astype(jnp.bfloat16)
    extended_normed = padded_2(normed, (("sp", 0),), 1)
    padded = jnp.pad(extended_normed, ((0, 0), (1, 1), (1, 1), (0, 0)))
    conv = conv_block(padded, plane_count, row_count, col_count, conv_weight)
    hidden = jax.nn.silu(conv).astype(jnp.bfloat16)
    reduced = down_block(hidden, down_weight)
    return reduced.astype(jnp.bfloat16)


def solution(mesh):
    in_specs = (P(("grp", "sp"), None, None, None), P(), P(), P(), P())
    out_specs = P(("grp", "sp"), None, None, None)
    return jax.shard_map(body, mesh=mesh, in_specs=in_specs, out_specs=out_specs, check_vma=False)
```

profile of v0, /device:TPU:1, one launch (start us, length us, event | category | flops | bytes accessed | tf_op | source)
XLA Modules:
  0.0 201.5 jit_solution(5176924969139679377)
XLA Ops:
  0.0 1.9 fusion.6
  2.3 30.6 %all-reduce.1 = (f32[32]{0:T(128)S(1)}, f32[32]{0:T(128)S(1)}) all-reduce(f32[32]{0:T(128)S(1)} %reduce_sum.37, f32[32]{0:T(128)S(1)} %reduce_sum.25), channel_id=1, replica_groups=mesh['grp'=2,'sp'=16] {'sp'}, use_global_device_ids=true, to_apply=%region_5.6 | all-reduce | flops 64 | bytes 512 | tf_op jit(solution)/shard_map/psum | solution.py:62
  33.2 0.7 multiply_subtract_fusion
  33.9 2.0 fusion.8
  36.0 3.0 %collective-permute-start = (bf16[1,32,48,256]{3,2,1,0:T(8,128)(2,1)S(1)}, bf16[1,32,48,256]{3,2,1,0:T(8,128)(2,1)S(1)}, u32[]{:S(2)}, u32[]{:S(2)}) collective-permute-start(bf16[1,32,48,256]{3,2,1,0:T(8,128)(2,1)S(1)} %get-tuple-element.11), channel_id=1, source_target_pairs={{0,1},{1,2},{2,3},{3,4},{4,5},{5,6},{6,7},{7,8},{8,9},{9,10},{10,1... | collective-permute-start | bytes 2359304 | tf_op jit(solution)/shard_map/ppermute | solution.py:14
  39.0 4.7 %collective-permute-start.1 = (bf16[1,32,48,256]{3,2,1,0:T(8,128)(2,1)S(1)}, bf16[1,32,48,256]{3,2,1,0:T(8,128)(2,1)S(1)}, u32[]{:S(2)}, u32[]{:S(2)}) collective-permute-start(bf16[1,32,48,256]{3,2,1,0:T(8,128)(2,1)S(1)} %get-tuple-element.12), channel_id=1, source_target_pairs={{1,0},{2,1},{3,2},{4,3},{5,4},{6,5},{7,6},{8,7},{9,8},{10,9},{11,1... | collective-permute-start | bytes 2359304 | tf_op jit(solution)/shard_map/ppermute | solution.py:17
  43.7 0.6 fusion.104
  44.2 12.1 %collective-permute-done = bf16[1,32,48,256]{3,2,1,0:T(8,128)(2,1)S(1)} collective-permute-done((bf16[1,32,48,256]{3,2,1,0:T(8,128)(2,1)S(1)}, bf16[1,32,48,256]{3,2,1,0:T(8,128)(2,1)S(1)}, u32[]{:S(2)}, u32[]{:S(2)}) %collective-permute-start) | collective-permute-done | bytes 786464 | tf_op jit(solution)/shard_map/ppermute | solution.py:14
  56.3 2.0 select_maximum_fusion
  58.3 2.6 %fusion.18 = f32[2,32,48,256]{3,2,1,0:T(8,128)} fusion(bf16[4,34,50,256]{3,2,1,0:T(8,128)(2,1)S(1)} %select_maximum_fusion, bf16[27,256,256]{2,1,0:T(8,128)(2,1)S(1)} %copy-done.1), kind=kOutput, calls=%fused_computation.28 | convolution fusion | flops 402653184 | bytes 4849664 | tf_op jit(solution)/shard_map/dhwc,ck->dhwk/dot_general | solution.py:34
  60.9 2.3 %fusion.20 = f32[2,32,48,256]{3,2,1,0:T(8,128)} fusion(bf16[4,34,50,256]{3,2,1,0:T(8,128)(2,1)S(1)} %select_maximum_fusion, bf16[27,256,256]{2,1,0:T(8,128)(2,1)S(1)} %copy-done.1), kind=kOutput, calls=%fused_computation.30 | convolution fusion | flops 402653184 | bytes 4849664 | tf_op jit(solution)/shard_map/dhwc,ck->dhwk/dot_general | solution.py:34
  63.2 2.3 %fusion.22 = f32[2,32,48,256]{3,2,1,0:T(8,128)} fusion(bf16[4,34,50,256]{3,2,1,0:T(8,128)(2,1)S(1)} %select_maximum_fusion, bf16[27,256,256]{2,1,0:T(8,128)(2,1)S(1)} %copy-done.1), kind=kOutput, calls=%fused_computation.32 | convolution fusion | flops 402653184 | bytes 4849664 | tf_op jit(solution)/shard_map/dhwc,ck->dhwk/dot_general | solution.py:34
  65.5 2.2 %fusion.24 = f32[2,32,48,256]{3,2,1,0:T(8,128)} fusion(bf16[4,34,50,256]{3,2,1,0:T(8,128)(2,1)S(1)} %select_maximum_fusion, bf16[27,256,256]{2,1,0:T(8,128)(2,1)S(1)} %copy-done.1), kind=kOutput, calls=%fused_computation.34 | convolution fusion | flops 402653184 | bytes 4849664 | tf_op jit(solution)/shard_map/dhwc,ck->dhwk/dot_general | solution.py:34
  67.7 2.3 %fusion.26 = f32[2,32,48,256]{3,2,1,0:T(8,128)} fusion(bf16[4,34,50,256]{3,2,1,0:T(8,128)(2,1)S(1)} %select_maximum_fusion, bf16[27,256,256]{2,1,0:T(8,128)(2,1)S(1)} %copy-done.1), kind=kOutput, calls=%fused_computation.36 | convolution fusion | flops 402653184 | bytes 4849664 | tf_op jit(solution)/shard_map/dhwc,ck->dhwk/dot_general | solution.py:34
  70.0 2.3 %fusion.28 = f32[2,32,48,256]{3,2,1,0:T(8,128)} fusion(bf16[4,34,50,256]{3,2,1,0:T(8,128)(2,1)S(1)} %select_maximum_fusion, bf16[27,256,256]{2,1,0:T(8,128)(2,1)S(1)} %copy-done.1), kind=kOutput, calls=%fused_computation.38 | convolution fusion | flops 402653184 | bytes 4849664 | tf_op jit(solution)/shard_map/dhwc,ck->dhwk/dot_general | solution.py:34
  72.3 2.2 %fusion.30 = f32[2,32,48,256]{3,2,1,0:T(8,128)} fusion(bf16[4,34,50,256]{3,2,1,0:T(8,128)(2,1)S(1)} %select_maximum_fusion, bf16[27,256,256]{2,1,0:T(8,128)(2,1)S(1)} %copy-done.1), kind=kOutput, calls=%fused_computation.40 | convolution fusion | flops 402653184 | bytes 4849664 | tf_op jit(solution)/shard_map/dhwc,ck->dhwk/dot_general | solution.py:34
  74.5 2.3 %fusion.32 = f32[2,32,48,256]{3,2,1,0:T(8,128)} fusion(bf16[4,34,50,256]{3,2,1,0:T(8,128)(2,1)S(1)} %select_maximum_fusion, bf16[27,256,256]{2,1,0:T(8,128)(2,1)S(1)} %copy-done.1), kind=kOutput, calls=%fused_computation.42 | convolution fusion | flops 402653184 | bytes 4849664 | tf_op jit(solution)/shard_map/dhwc,ck->dhwk/dot_general | solution.py:34
  76.7 2.2 %fusion.34 = f32[2,32,48,256]{3,2,1,0:T(8,128)} fusion(bf16[4,34,50,256]{3,2,1,0:T(8,128)(2,1)S(1)} %select_maximum_fusion, bf16[27,256,256]{2,1,0:T(8,128)(2,1)S(1)} %copy-done.1), kind=kOutput, calls=%fused_computation.44 | convolution fusion | flops 402653184 | bytes 4849664 | tf_op jit(solution)/shard_map/dhwc,ck->dhwk/dot_general | solution.py:34
  79.0 2.3 %fusion.36 = f32[2,32,48,256]{3,2,1,0:T(8,128)} fusion(bf16[4,34,50,256]{3,2,1,0:T(8,128)(2,1)S(1)} %select_maximum_fusion, bf16[27,256,256]{2,1,0:T(8,128)(2,1)S(1)} %copy-done.1), kind=kOutput, calls=%fused_computation.46 | convolution fusion | flops 402653184 | bytes 4849664 | tf_op jit(solution)/shard_map/dhwc,ck->dhwk/dot_general | solution.py:34
  81.2 2.2 %fusion.38 = f32[2,32,48,256]{3,2,1,0:T(8,128)} fusion(bf16[4,34,50,256]{3,2,1,0:T(8,128)(2,1)S(1)} %select_maximum_fusion, bf16[27,256,256]{2,1,0:T(8,128)(2,1)S(1)} %copy-done.1), kind=kOutput, calls=%fused_computation.48 | convolution fusion | flops 402653184 | bytes 4849664 | tf_op jit(solution)/shard_map/dhwc,ck->dhwk/dot_general | solution.py:34
  83.4 2.2 %fusion.40 = f32[2,32,48,256]{3,2,1,0:T(8,128)} fusion(bf16[4,34,50,256]{3,2,1,0:T(8,128)(2,1)S(1)} %select_maximum_fusion, bf16[27,256,256]{2,1,0:T(8,128)(2,1)S(1)} %copy-done.1), kind=kOutput, calls=%fused_computation.50 | convolution fusion | flops 402653184 | bytes 4849664 | tf_op jit(solution)/shard_map/dhwc,ck->dhwk/dot_general | solution.py:34
  85.7 2.3 %fusion.42 = f32[2,32,48,256]{3,2,1,0:T(8,128)} fusion(bf16[4,34,50,256]{3,2,1,0:T(8,128)(2,1)S(1)} %select_maximum_fusion, bf16[27,256,256]{2,1,0:T(8,128)(2,1)S(1)} %copy-done.1), kind=kOutput, calls=%fused_computation.52 | convolution fusion | flops 402653184 | bytes 4849664 | tf_op jit(solution)/shard_map/dhwc,ck->dhwk/dot_general | solution.py:34
  88.0 2.3 %fusion.44 = f32[2,32,48,256]{3,2,1,0:T(8,128)} fusion(bf16[4,34,50,256]{3,2,1,0:T(8,128)(2,1)S(1)} %select_maximum_fusion, bf16[27,256,256]{2,1,0:T(8,128)(2,1)S(1)} %copy-done.1), kind=kOutput, calls=%fused_computation.54 | convolution fusion | flops 402653184 | bytes 4849664 | tf_op jit(solution)/shard_map/dhwc,ck->dhwk/dot_general | solution.py:34
  90.3 2.3 %fusion.46 = f32[2,32,48,256]{3,2,1,0:T(8,128)} fusion(bf16[4,34,50,256]{3,2,1,0:T(8,128)(2,1)S(1)} %select_maximum_fusion, bf16[27,256,256]{2,1,0:T(8,128)(2,1)S(1)} %copy-done.1), kind=kOutput, calls=%fused_computation.56 | convolution fusion | flops 402653184 | bytes 4849664 | tf_op jit(solution)/shard_map/dhwc,ck->dhwk/dot_general | solution.py:34
  92.6 2.2 %fusion.48 = f32[2,32,48,256]{3,2,1,0:T(8,128)} fusion(bf16[4,34,50,256]{3,2,1,0:T(8,128)(2,1)S(1)} %select_maximum_fusion, bf16[27,256,256]{2,1,0:T(8,128)(2,1)S(1)} %copy-done.1), kind=kOutput, calls=%fused_computation.58 | convolution fusion | flops 402653184 | bytes 4849664 | tf_op jit(solution)/shard_map/dhwc,ck->dhwk/dot_general | solution.py:34
  94.8 2.2 %fusion.50 = f32[2,32,48,256]{3,2,1,0:T(8,128)} fusion(bf16[4,34,50,256]{3,2,1,0:T(8,128)(2,1)S(1)} %select_maximum_fusion, bf16[27,256,256]{2,1,0:T(8,128)(2,1)S(1)} %copy-done.1), kind=kOutput, calls=%fused_computation.60 | convolution fusion | flops 402653184 | bytes 4849664 | tf_op jit(solution)/shard_map/dhwc,ck->dhwk/dot_general | solution.py:34
  97.0 2.2 %fusion.52 = f32[2,32,48,256]{3,2,1,0:T(8,128)} fusion(bf16[4,34,50,256]{3,2,1,0:T(8,128)(2,1)S(1)} %select_maximum_fusion, bf16[27,256,256]{2,1,0:T(8,128)(2,1)S(1)} %copy-done.1), kind=kOutput, calls=%fused_computation.62 | convolution fusion | flops 402653184 | bytes 4849664 | tf_op jit(solution)/shard_map/dhwc,ck->dhwk/dot_general | solution.py:34
  99.3 2.2 %fusion.54 = f32[2,32,48,256]{3,2,1,0:T(8,128)} fusion(bf16[4,34,50,256]{3,2,1,0:T(8,128)(2,1)S(1)} %select_maximum_fusion, bf16[27,256,256]{2,1,0:T(8,128)(2,1)S(1)} %copy-done.1), kind=kOutput, calls=%fused_computation.64 | convolution fusion | flops 402653184 | bytes 4849664 | tf_op jit(solution)/shard_map/dhwc,ck->dhwk/dot_general | solution.py:34
  101.5 2.3 %fusion.56 = f32[2,32,48,256]{3,2,1,0:T(8,128)} fusion(bf16[4,34,50,256]{3,2,1,0:T(8,128)(2,1)S(1)} %select_maximum_fusion, bf16[27,256,256]{2,1,0:T(8,128)(2,1)S(1)} %copy-done.1), kind=kOutput, calls=%fused_computation.66 | convolution fusion | flops 402653184 | bytes 4849664 | tf_op jit(solution)/shard_map/dhwc,ck->dhwk/dot_general | solution.py:34
  103.8 2.2 %fusion.58 = f32[2,32,48,256]{3,2,1,0:T(8,128)} fusion(bf16[4,34,50,256]{3,2,1,0:T(8,128)(2,1)S(1)} %select_maximum_fusion, bf16[27,256,256]{2,1,0:T(8,128)(2,1)S(1)} %copy-done.1), kind=kOutput, calls=%fused_computation.68 | convolution fusion | flops 402653184 | bytes 4849664 | tf_op jit(solution)/shard_map/dhwc,ck->dhwk/dot_general | solution.py:34
  106.0 2.3 %fusion.60 = f32[2,32,48,256]{3,2,1,0:T(8,128)} fusion(bf16[4,34,50,256]{3,2,1,0:T(8,128)(2,1)S(1)} %select_maximum_fusion, bf16[27,256,256]{2,1,0:T(8,128)(2,1)S(1)} %copy-done.1), kind=kOutput, calls=%fused_computation.70 | convolution fusion | flops 402653184 | bytes 4849664 | tf_op jit(solution)/shard_map/dhwc,ck->dhwk/dot_general | solution.py:34
  108.4 2.2 %fusion.62 = f32[2,32,48,256]{3,2,1,0:T(8,128)} fusion(bf16[4,34,50,256]{3,2,1,0:T(8,128)(2,1)S(1)} %select_maximum_fusion, bf16[27,256,256]{2,1,0:T(8,128)(2,1)S(1)} %copy-done.1), kind=kOutput, calls=%fused_computation.72 | convolution fusion | flops 402653184 | bytes 4849664 | tf_op jit(solution)/shard_map/dhwc,ck->dhwk/dot_general | solution.py:34
  110.6 2.2 %fusion.13 = f32[2,32,48,256]{3,2,1,0:T(8,128)} fusion(bf16[1,32,48,256]{3,2,1,0:T(8,128)(2,1)S(1)} %collective-permute-done.1, bf16[2,32,48,256]{3,2,1,0:T(8,128)(2,1)S(1)} %fusion.8, bf16[27,256,256]{2,1,0:T(8,128)(2,1)S(1)} %copy-done.1), kind=kOutput, calls=%fused_computation.23 | convolution fusion | flops 407371776 | bytes 5636096 | tf_op jit(solution)/shard_map/dhwc,ck->dhwk/dot_general | solution.py:34
  112.8 2.3 %fusion.9 = f32[2,32,48,256]{3,2,1,0:T(8,128)} fusion(bf16[2,32,48,256]{3,2,1,0:T(8,128)(2,1)S(1)} %fusion.8, bf16[1,32,48,256]{3,2,1,0:T(8,128)(2,1)S(1)} %collective-permute-done, bf16[27,256,256]{2,1,0:T(8,128)(2,1)S(1)} %copy-done.1), kind=kOutput, calls=%fused_computation.19 | convolution fusion | flops 407371776 | bytes 5636096 | tf_op jit(solution)/shard_map/dhwc,ck->dhwk/dot_general | solution.py:34
  115.1 27.5 %multiply_convert_fusion = bf16[2,32,48,256]{3,2,1,0:T(8,128)(2,1)} fusion(f32[2,32,48,256]{3,2,1,0:T(8,128)} %fusion.18, f32[2,32,48,256]{3,2,1,0:T(8,128)} %fusion.20, f32[2,32,48,256]{3,2,1,0:T(8,128)} %fusion.22, f32[2,32,48,256]{3,2,1,0:T(8,128)} %fusion.13, f32[2,32,48,256]{3,2,1,0:T(8,128)} %fusion.24, f32[2,32,48,256]{3,2,1,0:T(8,128)} %fusion.26, ...), kind=kOutput, calls=%fused_computation.18 | convolution fusion | flops 427032576 | bytes 85065728 | tf_op jit(solution)/shard_map/dhwc,ck->dhwk/dot_general | solution.py:34
  142.5 6.8 %slice.296 = bf16[1,16,24,256]{3,2,1,0:T(8,128)(2,1)S(1)} slice(bf16[2,32,48,256]{3,2,1,0:T(8,128)(2,1)} %multiply_convert_fusion), slice={[1:2:1], [1:32:2], [1:48:2], [0:256:1]} | slice | bytes 393216 | tf_op jit(solution)/shard_map/slice | solution.py:47
  149.3 6.6 %slice.294 = bf16[1,16,24,256]{3,2,1,0:T(8,128)(2,1)S(1)} slice(bf16[2,32,48,256]{3,2,1,0:T(8,128)(2,1)} %multiply_convert_fusion), slice={[1:2:1], [1:32:2], [0:48:2], [0:256:1]} | slice | bytes 393216 | tf_op jit(solution)/shard_map/slice | solution.py:47
  155.9 6.6 %slice.292 = bf16[1,16,24,256]{3,2,1,0:T(8,128)(2,1)S(1)} slice(bf16[2,32,48,256]{3,2,1,0:T(8,128)(2,1)} %multiply_convert_fusion), slice={[1:2:1], [0:32:2], [1:48:2], [0:256:1]} | slice | bytes 393216 | tf_op jit(solution)/shard_map/slice | solution.py:47
  162.6 6.6 %slice.290 = bf16[1,16,24,256]{3,2,1,0:T(8,128)(2,1)S(1)} slice(bf16[2,32,48,256]{3,2,1,0:T(8,128)(2,1)} %multiply_convert_fusion), slice={[1:2:1], [0:32:2], [0:48:2], [0:256:1]} | slice | bytes 393216 | tf_op jit(solution)/shard_map/slice | solution.py:47
  169.2 6.6 %slice.288 = bf16[1,16,24,256]{3,2,1,0:T(8,128)(2,1)S(1)} slice(bf16[2,32,48,256]{3,2,1,0:T(8,128)(2,1)} %multiply_convert_fusion), slice={[0:1:1], [1:32:2], [1:48:2], [0:256:1]} | slice | bytes 393216 | tf_op jit(solution)/shard_map/slice | solution.py:47
  175.8 6.6 %slice.286 = bf16[1,16,24,256]{3,2,1,0:T(8,128)(2,1)S(1)} slice(bf16[2,32,48,256]{3,2,1,0:T(8,128)(2,1)} %multiply_convert_fusion), slice={[0:1:1], [1:32:2], [0:48:2], [0:256:1]} | slice | bytes 393216 | tf_op jit(solution)/shard_map/slice | solution.py:47
  182.4 8.5 %slice.284 = bf16[1,16,24,256]{3,2,1,0:T(8,128)(2,1)} slice(bf16[2,32,48,256]{3,2,1,0:T(8,128)(2,1)} %multiply_convert_fusion), slice={[0:1:1], [0:32:2], [1:48:2], [0:256:1]} | slice | bytes 393216 | tf_op jit(solution)/shard_map/slice | solution.py:47
  190.9 6.6 %slice.282 = bf16[1,16,24,256]{3,2,1,0:T(8,128)(2,1)S(1)} slice(bf16[2,32,48,256]{3,2,1,0:T(8,128)(2,1)} %multiply_convert_fusion), slice={[0:1:1], [0:32:2], [0:48:2], [0:256:1]} | slice | bytes 393216 | tf_op jit(solution)/shard_map/slice | solution.py:47
  197.8 1.2 convolution_add_fusion.6
  199.3 0.3 convolution_add_fusion.4
  199.6 0.3 convolution_add_fusion.3
  199.9 0.3 convolution_add_fusion.2
  200.5 1.0 fusion.65
  (20 shorter events, 1.7 us)
Async XLA Ops:
  33.9 9.7 %copy-start.1 = (bf16[27,256,256]{2,1,0:T(8,128)(2,1)S(1)}, bf16[27,256,256]{2,1,0:T(8,128)(2,1)}, u32[]{:S(2)}) copy-start(bf16[27,256,256]{2,1,0:T(8,128)(2,1)} %param.8) | copy-start | bytes 10616836
  36.0 20.3 %collective-permute-start = (bf16[1,32,48,256]{3,2,1,0:T(8,128)(2,1)S(1)}, bf16[1,32,48,256]{3,2,1,0:T(8,128)(2,1)S(1)}, u32[]{:S(2)}, u32[]{:S(2)}) collective-permute-start(bf16[1,32,48,256]{3,2,1,0:T(8,128)(2,1)S(1)} %get-tuple-element.11), channel_id=1, source_target_pairs={{0,1},{1,2},{2,3},{3,4},{4,5},{5,6},{6,7},{7,8},{8,9},{9,10},{10,1... | collective-permute-start | bytes 2359304 | tf_op jit(solution)/shard_map/ppermute | solution.py:14
  39.0 17.3 %collective-permute-start.1 = (bf16[1,32,48,256]{3,2,1,0:T(8,128)(2,1)S(1)}, bf16[1,32,48,256]{3,2,1,0:T(8,128)(2,1)S(1)}, u32[]{:S(2)}, u32[]{:S(2)}) collective-permute-start(bf16[1,32,48,256]{3,2,1,0:T(8,128)(2,1)S(1)} %get-tuple-element.12), channel_id=1, source_target_pairs={{1,0},{2,1},{3,2},{4,3},{5,4},{6,5},{7,6},{8,7},{9,8},{10,9},{11,1... | collective-permute-start | bytes 2359304 | tf_op jit(solution)/shard_map/ppermute | solution.py:17
  58.3 50.1 %copy-start = (bf16[4,34,50,256]{3,2,1,0:T(8,128)(2,1)}, bf16[4,34,50,256]{3,2,1,0:T(8,128)(2,1)S(1)}, u32[]{:S(2)}) copy-start(bf16[4,34,50,256]{3,2,1,0:T(8,128)(2,1)S(1)} %select_maximum_fusion) | copy-start | bytes 10444804
  142.5 55.0 %copy-start.2 = (bf16[8,256,512]{2,1,0:T(8,128)(2,1)S(1)}, bf16[8,256,512]{2,1,0:T(8,128)(2,1)}, u32[]{:S(2)}) copy-start(bf16[8,256,512]{2,1,0:T(8,128)(2,1)} %param.9) | copy-start | bytes 6291460
where the time goes:
time: 206 us; the launch traced here: 201 us
  matrix products  88.6 us (43%)
  local copies, waits for them, and re-layouts  55.6 us (27%)
  blocking collectives  30.6 us (15%)
  waiting for transfers between devices  12.1 us (6%)
  starting transfers between devices  7.65 us (4%)
  other arithmetic  6.75 us (3%)
    dot_general x27, matrix products, conv_block(): jnp.einsum('dhwc,ck->dhwk', window, filters[tap_index], preferred_element...  84.8 us
    slice x8, local copies, waits for them, and re-layouts, down_block(): window = hidden[shift_d::2, shift_h::2, shift_w::2, :]  55 us
    psum x1, blocking collectives, body(): total, squares = lax.psum((local_total, local_squares), 'sp')  30.6 us
    ppermute x1, waiting for transfers between devices, padded_2(): lax.ppermute(lax.slice_in_dim(block, block.shape[dim] - width, None, axis...  12.1 us
    ppermute x1, starting transfers between devices, padded_2(): lax.ppermute(lax.slice_in_dim(block, 0, width, axis=dim), axis, backward)  4.67 us
  transfers between devices with their start and end apart: 2, of which 1 were waited for; matrix products, arithmetic and copies ran while one was open for 0% of the time, Pallas kernels for 0%

commit v1 on v0

v1 whole, which is shorter than its diff:
```python
import functools

import jax
import jax.numpy as jnp
from jax import lax
from jax.experimental import pallas as pl
from jax.experimental.pallas import tpu as pltpu
from jax.sharding import PartitionSpec as P

GROUPS = 32
LANES = 128
ROWS = 8
NROWS = 2
MESH = pl.DeviceIdType.MESH


def kernel(
    count,
    vol_hbm, gain_ref, bias_ref, conv_hbm, down_hbm,
    out_ref,
    vol, low, high, conv_w, down_w, taps, acc, slots,
    vol_sem, w_sem, halo_send, halo_recv, stat_send, stat_recv,
):
    planes, height, width, chans = vol.shape
    me = lax.axis_index("sp")

    barrier = pltpu.get_barrier_semaphore()

    def greet(k, _):
        pl.semaphore_signal(
            barrier, inc=1, device_id={"sp": lax.rem(me + k, count)}, device_id_type=MESH
        )
        return 0

    lax.fori_loop(1, count, greet, 0)
    vol_copies = [
        pltpu.make_async_copy(vol_hbm.at[p], vol.at[p], vol_sem.at[p]) for p in range(planes)
    ]
    for copy in vol_copies:
        copy.start()
    conv_copy = pltpu.make_async_copy(conv_hbm, conv_w, w_sem.at[0])
    down_copy = pltpu.make_async_copy(down_hbm, down_w, w_sem.at[1])
    conv_copy.start()
    down_copy.start()
    pl.semaphore_wait(barrier, count - 1)

    up = pltpu.make_async_remote_copy(
        vol_hbm.at[planes - 1], low, halo_send.at[0], halo_recv.at[0],
        device_id={"sp": lax.rem(me + 1, count)}, device_id_type=MESH,
    )
    down = pltpu.make_async_remote_copy(
        vol_hbm.at[0], high, halo_send.at[1], halo_recv.at[1],
        device_id={"sp": lax.rem(me + count - 1, count)}, device_id_type=MESH,
    )

    @pl.when(me < count - 1)
    def _():
        up.start()

    @pl.when(me > 0)
    def _():
        down.start()

    srows = 2
    zero = jnp.zeros((8, chans), jnp.float32)
    sums = (zero, zero)
    for p in range(planes):
        vol_copies[p].wait()

        def add(i, carry, p=p):
            total, squares = carry
            block = vol[p, pl.ds(i * srows, srows)].astype(jnp.float32)
            block = block.reshape(srows * width // 8, 8, chans)
            return total + jnp.sum(block, axis=0), squares + jnp.sum(block * block, axis=0)

        sums = lax.fori_loop(0, height // srows, add, sums, unroll=4)
    row = lax.broadcasted_iota(jnp.int32, (8, chans), 0)
    slots[me] = jnp.where(
        row == 0,
        jnp.sum(sums[0], axis=0, keepdims=True),
        jnp.where(row == 1, jnp.sum(sums[1], axis=0, keepdims=True), 0.0),
    )

    def stat_copy(k):
        return pltpu.make_async_remote_copy(
            slots.at[me], slots.at[me], stat_send.at[k], stat_recv.at[me],
            device_id={"sp": lax.rem(me + k, count)}, device_id_type=MESH,
        )

    def send(k, _):
        stat_copy(k).start()
        return 0

    lax.fori_loop(1, count, send, 0)

    edge = jnp.zeros((planes + 2, 1, width, 3 * chans), jnp.bfloat16)
    taps[:, 0:1] = edge
    taps[:, height + 1 : height + 2] = edge

    def receive(k, _):
        source = lax.rem(me + k, count)
        pltpu.make_async_remote_copy(
            slots.at[source], slots.at[source], stat_send.at[k], stat_recv.at[source],
            device_id={"sp": source}, device_id_type=MESH,
        ).wait_recv()
        return 0

    lax.fori_loop(1, count, receive, 0)
    total = jnp.sum(slots[...], axis=0)
    per_group = chans // GROUPS
    lane = lax.broadcasted_iota(jnp.int32, (8, chans), 1)
    step = 1
    while step < per_group:
        other = jnp.where(
            (lane & step) == 0,
            pltpu.roll(total, chans - step, 1),
            pltpu.roll(total, step, 1),
        )
        total = total + other
        step *= 2
    cells = planes * count * height * width * per_group
    mean = total[0:1] * (1.0 / cells)
    var = total[1:2] * (1.0 / cells) - mean * mean
    scale = gain_ref[...] * lax.rsqrt(var + 1e-05)
    shift = bias_ref[...] - mean * scale

    nrow = lax.broadcasted_iota(jnp.int32, (NROWS * width, chans), 0)
    first = nrow == 0
    last = nrow == width - 1
    for r in range(1, NROWS):
        first = first | (nrow == r * width)
        last = last | (nrow == r * width + width - 1)

    def normalise(source, plane):
        def one(i, _):
            h = i * NROWS
            block = source[pl.ds(h, NROWS)].astype(jnp.float32)
            block = block.reshape(NROWS * width, chans) * scale + shift
            before = jnp.where(first, 0.0, pltpu.roll(block, 1, 0))
            after = jnp.where(last, 0.0, pltpu.roll(block, NROWS * width - 1, 0))
            for c, value in enumerate((before, block, after)):
                taps[plane, pl.ds(h + 1, NROWS), :, c * chans : (c + 1) * chans] = value.astype(
                    jnp.bfloat16
                ).reshape(NROWS, width, chans)
            return 0

        lax.fori_loop(0, height // NROWS, one, 0, unroll=2)

    for p in range(planes):
        normalise(vol.at[p], p + 1)
    conv_copy.wait()

    def window(plane, h):
        return jnp.concatenate(
            [
                taps[plane, pl.ds(h + b, ROWS)].reshape(ROWS * width, 3 * chans)
                for b in range(3)
            ],
            axis=1,
        )

    def weight(a):
        return conv_w[9 * a : 9 * a + 9].reshape(9 * chans, chans)

    def inner(i, _):
        h = i * ROWS
        lhs = [window(p + 1, h) for p in range(2)]
        for out in range(2):
            value = jnp.dot(lhs[0], weight(1 - out), preferred_element_type=jnp.float32)
            value += jnp.dot(lhs[1], weight(2 - out), preferred_element_type=jnp.float32)
            value = value.reshape(ROWS, width, chans)
            for part in range(chans // LANES):
                acc[part, out, pl.ds(h, ROWS)] = value[:, :, part * LANES : (part + 1) * LANES]
        return 0

    lax.fori_loop(0, height // ROWS, inner, 0)

    @pl.when(me > 0)
    def _():
        up.wait_recv()
        normalise(low, 0)

    @pl.when(me == 0)
    def _():
        taps[0] = jnp.zeros(taps.shape[1:], jnp.bfloat16)

    @pl.when(me < count - 1)
    def _():
        down.wait_recv()
        normalise(high, planes + 1)

    @pl.when(me == count - 1)
    def _():
        taps[planes + 1] = jnp.zeros(taps.shape[1:], jnp.bfloat16)

    def outer(i, _):
        h = i * ROWS
        for out in range(2):
            value = jnp.dot(
                window(3 * out, h), weight(2 * out), preferred_element_type=jnp.float32
            ).reshape(ROWS, width, chans)
            for part in range(chans // LANES):
                half = value[:, :, part * LANES : (part + 1) * LANES]
                half = 0.5 * (half + acc[part, out, pl.ds(h, ROWS)])
                acc[part, out, pl.ds(h, ROWS)] = half + half * jnp.tanh(half)
        return 0

    lax.fori_loop(0, height // ROWS, outer, 0)

    down_copy.wait()
    hidden = acc.reshape(chans // LANES, 2, height // 2, 2 * width, LANES)
    pieces = []
    for a in range(2):
        for b in range(2):
            for c in range(2):
                for part in range(chans // LANES):
                    piece = hidden[part, a, :, pl.ds(b * width + c, width // 2, stride=2), :]
                    pieces.append(
                        piece.reshape(height // 2 * (width // 2), LANES).astype(jnp.bfloat16)
                    )
    result = jnp.dot(
        jnp.concatenate(pieces, axis=1),
        down_w[...].reshape(8 * chans, down_w.shape[2]),
        preferred_element_type=jnp.float32,
    )
    out_ref[...] = result.astype(jnp.bfloat16).reshape(out_ref.shape)

    @pl.when(me < count - 1)
    def _():
        up.wait_send()

    @pl.when(me > 0)
    def _():
        down.wait_send()

    def sent(k, _):
        stat_copy(k).wait_send()
        return 0

    lax.fori_loop(1, count, sent, 0)


def body(volume, norm_gain, norm_bias, conv_weight, down_weight):
    planes, height, width, chans = volume.shape
    count = lax.axis_size("sp")
    chans2 = down_weight.shape[2]
    return pl.pallas_call(
        functools.partial(kernel, count),
        out_shape=jax.ShapeDtypeStruct((planes // 2, height // 2, width // 2, chans2), jnp.bfloat16),
        in_specs=[
            pl.BlockSpec(memory_space=pl.ANY),
            pl.BlockSpec(memory_space=pltpu.VMEM),
            pl.BlockSpec(memory_space=pltpu.VMEM),
            pl.BlockSpec(memory_space=pl.ANY),
            pl.BlockSpec(memory_space=pl.ANY),
        ],
        out_specs=pl.BlockSpec(memory_space=pltpu.VMEM),
        scratch_shapes=[
            pltpu.VMEM((planes, height, width, chans), jnp.bfloat16),
            pltpu.VMEM((height, width, chans), jnp.bfloat16),
            pltpu.VMEM((height, width, chans), jnp.bfloat16),
            pltpu.VMEM(conv_weight.shape, jnp.bfloat16),
            pltpu.VMEM(down_weight.shape, jnp.bfloat16),
            pltpu.VMEM((planes + 2, height + 2, width, 3 * chans), jnp.bfloat16),
            pltpu.VMEM((chans // LANES, 2, height, width, LANES), jnp.float32),
            pltpu.VMEM((count, 8, chans), jnp.float32),
            pltpu.SemaphoreType.DMA((planes,)),
            pltpu.SemaphoreType.DMA((2,)),
            pltpu.SemaphoreType.DMA((2,)),
            pltpu.SemaphoreType.DMA((2,)),
            pltpu.SemaphoreType.DMA((count,)),
            pltpu.SemaphoreType.DMA((count,)),
        ],
        compiler_params=pltpu.CompilerParams(
            collective_id=0, has_side_effects=True, vmem_limit_bytes=56 * 2**20
        ),
        name="encoder",
    )(volume, norm_gain.reshape(1, chans), norm_bias.reshape(1, chans), conv_weight, down_weight)


def solution(mesh):
    in_specs = (P(("grp", "sp"), None, None, None), P(), P(), P(), P())
    out_specs = P(("grp", "sp"), None, None, None)
    return jax.shard_map(body, mesh=mesh, in_specs=in_specs, out_specs=out_specs, check_vma=False)
```

time: 206 us -> 44.2 us (0.21)
  the two profiles are of different devices: /device:TPU:1 before, /device:TPU:5 now
where the time goes in v1:
time: 44.2 us; the launch traced here: 44 us
  Pallas kernels  42.2 us (95%)
  local copies, waits for them, and re-layouts  1.77 us (4%)
    pallas_call x1, Pallas kernels, body(): pl.pallas_call(functools.partial(kernel, count), out_shape=jax.ShapeDtype...  42.2 us
    unnamed x1, local copies, waits for them, and re-layouts  1.77 us

profile of v1, /device:TPU:5, one launch (start us, length us, event | category | flops | bytes accessed | tf_op | source)
XLA Modules:
  0.0 44.0 jit_solution(3934465244223095145)
XLA Ops:
  0.0 42.2 %encoder.1 = bf16[1,16,24,512]{3,2,1,0:T(8,128)(2,1)} custom-call(bf16[2,32,48,256]{3,2,1,0:T(8,128)(2,1)} %vol_hbm.1, f32[1,256]{1,0:T(1,128)} %bitcast.2, f32[1,256]{1,0:T(1,128)} %bitcast.3, bf16[27,256,256]{2,1,0:T(8,128)(2,1)} %conv_hbm.1, bf16[8,256,512]{2,1,0:T(8,128)(2,1)} %down_hbm.1), custom_call_target="tpu_custom_call" | custom-call | tf_op jit(solution)/shard_map/encoder/pallas_call | solution.py:247
  42.2 1.8 %copy.7 = bf16[1,16,24,512]{3,2,1,0:T(8,128)(2,1)} copy(bf16[1,16,24,512]{3,2,1,0:T(8,128)(2,1)} %encoder.1) | data formatting | bytes 786432

commit v2 on v1

--- a/solution.py
+++ b/solution.py
@@ -10,6 +10,7 @@
 GROUPS = 32
 LANES = 128
 ROWS = 8
+CHUNK = 8
 NROWS = 2
 MESH = pl.DeviceIdType.MESH
 
@@ -18,8 +19,8 @@
     count,
     vol_hbm, gain_ref, bias_ref, conv_hbm, down_hbm,
     out_ref,
-    vol, low, high, conv_w, down_w, taps, acc, slots,
-    vol_sem, w_sem, halo_send, halo_recv, stat_send, stat_recv,
+    vol, near, far, conv_w, down_w, taps, acc, slots,
+    vol_sem, w_sem, near_sem, far_send, far_recv, stat_send, stat_recv,
 ):
     planes, height, width, chans = vol.shape
     me = lax.axis_index("sp")
@@ -44,22 +45,22 @@
     down_copy.start()
     pl.semaphore_wait(barrier, count - 1)
 
-    up = pltpu.make_async_remote_copy(
-        vol_hbm.at[planes - 1], low, halo_send.at[0], halo_recv.at[0],
-        device_id={"sp": lax.rem(me + 1, count)}, device_id_type=MESH,
+    odd = lax.rem(me, 2)
+    even = 1 - odd
+    has_far = jnp.logical_and(me > 0, me < count - 1)
+    far_device = lax.rem(me + 2 * odd - 1 + count, count)
+    near_copy = pltpu.make_async_remote_copy(
+        vol_hbm.at[even], near, near_sem.at[0], near_sem.at[1],
+        device_id={"sp": me + 1 - 2 * odd}, device_id_type=MESH,
     )
-    down = pltpu.make_async_remote_copy(
-        vol_hbm.at[0], high, halo_send.at[1], halo_recv.at[1],
-        device_id={"sp": lax.rem(me + count - 1, count)}, device_id_type=MESH,
-    )
-
-    @pl.when(me < count - 1)
-    def _():
-        up.start()
-
-    @pl.when(me > 0)
-    def _():
-        down.start()
+    far_copies = [
+        pltpu.make_async_remote_copy(
+            vol_hbm.at[odd, pl.ds(k * CHUNK, CHUNK)], far.at[pl.ds(k * CHUNK, CHUNK)],
+            far_send.at[k], far_recv.at[k],
+            device_id={"sp": far_device}, device_id_type=MESH,
+        )
+        for k in range(height // CHUNK)
+    ]
 
     srows = 2
     zero = jnp.zeros((8, chans), jnp.float32)
@@ -92,6 +93,13 @@
         return 0
 
     lax.fori_loop(1, count, send, 0)
+
+    near_copy.start()
+
+    @pl.when(has_far)
+    def _():
+        for copy in far_copies:
+            copy.start()
 
     edge = jnp.zeros((planes + 2, 1, width, 3 * chans), jnp.bfloat16)
     taps[:, 0:1] = edge
@@ -131,7 +139,7 @@
         first = first | (nrow == r * width)
         last = last | (nrow == r * width + width - 1)
 
-    def normalise(source, plane):
+    def normalise(source, plane, start, stop):
         def one(i, _):
             h = i * NROWS
             block = source[pl.ds(h, NROWS)].astype(jnp.float32)
@@ -144,27 +152,27 @@
                 ).reshape(NROWS, width, chans)
             return 0
 
-        lax.fori_loop(0, height // NROWS, one, 0, unroll=2)
+        lax.fori_loop(start // NROWS, stop // NROWS, one, 0, unroll=2)
 
     for p in range(planes):
-        normalise(vol.at[p], p + 1)
+        normalise(vol.at[p], p + 1, 0, height)
     conv_copy.wait()
 
-    def window(plane, h):
+    def window(plane, h, rows):
         return jnp.concatenate(
             [
-                taps[plane, pl.ds(h + b, ROWS)].reshape(ROWS * width, 3 * chans)
+                taps[plane, pl.ds(h + b, rows)].reshape(rows * width, 3 * chans)
                 for b in range(3)
             ],
             axis=1,
         )
 
     def weight(a):
-        return conv_w[9 * a : 9 * a + 9].reshape(9 * chans, chans)
+        return conv_w[pl.ds(9 * a, 9)].reshape(9 * chans, chans)
 
     def inner(i, _):
         h = i * ROWS
-        lhs = [window(p + 1, h) for p in range(2)]
+        lhs = [window(p + 1, h, ROWS) for p in range(2)]
         for out in range(2):
             value = jnp.dot(lhs[0], weight(1 - out), preferred_element_type=jnp.float32)
             value += jnp.dot(lhs[1], weight(2 - out), preferred_element_type=jnp.float32)
@@ -175,37 +183,40 @@
 
     lax.fori_loop(0, height // ROWS, inner, 0)
 
-    @pl.when(me > 0)
+    def finish(out, h, rows):
+        value = jnp.dot(
+            window(3 * out, h, rows), weight(2 * out), preferred_element_type=jnp.float32
+        ).reshape(rows, width, chans)
+        for part in range(chans // LANES):
+            half = value[:, :, part * LANES : (part + 1) * LANES]
+            half = 0.5 * (half + acc[part, out, pl.ds(h, rows)])
+            acc[part, out, pl.ds(h, rows)] = half + half * jnp.tanh(half)
+
+    near_copy.wait_recv()
+    normalise(near, 3 * even, 0, height)
+
+    def outer(i, _):
+        finish(even, i * ROWS, ROWS)
+        return 0
+
+    lax.fori_loop(0, height // ROWS, outer, 0)
+
+    @pl.when(jnp.logical_not(has_far))
     def _():
-        up.wait_recv()
-        normalise(low, 0)
-
-    @pl.when(me == 0)
-    def _():
-        taps[0] = jnp.zeros(taps.shape[1:], jnp.bfloat16)
-
-    @pl.when(me < count - 1)
-    def _():
-        down.wait_recv()
-        normalise(high, planes + 1)
-
-    @pl.when(me == count - 1)
-    def _():
-        taps[planes + 1] = jnp.zeros(taps.shape[1:], jnp.bfloat16)
-
-    def outer(i, _):
-        h = i * ROWS
-        for out in range(2):
-            value = jnp.dot(
-                window(3 * out, h), weight(2 * out), preferred_element_type=jnp.float32
-            ).reshape(ROWS, width, chans)
-            for part in range(chans // LANES):
-                half = value[:, :, part * LANES : (part + 1) * LANES]
-                half = 0.5 * (half + acc[part, out, pl.ds(h, ROWS)])
-                acc[part, out, pl.ds(h, ROWS)] = half + half * jnp.tanh(half)
-        return 0
-
-    lax.fori_loop(0, height // ROWS, outer, 0)
+        taps[3 * odd] = jnp.zeros(taps.shape[1:], jnp.bfloat16)
+
+    done = 0
+    for k, copy in enumerate(far_copies):
+        ready = (k + 1) * CHUNK
+
+        @pl.when(has_far)
+        def _():
+            copy.wait_recv()
+            normalise(far, 3 * odd, k * CHUNK, ready)
+
+        until = height if ready == height else ready - 1
+        finish(odd, done, until - done)
+        done = until
 
     down_copy.wait()
     hidden = acc.reshape(chans // LANES, 2, height // 2, 2 * width, LANES)
@@ -225,13 +236,12 @@
     )
     out_ref[...] = result.astype(jnp.bfloat16).reshape(out_ref.shape)
 
-    @pl.when(me < count - 1)
+    near_copy.wait_send()
+
+    @pl.when(has_far)
     def _():
-        up.wait_send()
-
-    @pl.when(me > 0)
-    def _():
-        down.wait_send()
+        for copy in far_copies:
+            copy.wait_send()
 
     def sent(k, _):
         stat_copy(k).wait_send()
@@ -267,7 +277,8 @@
             pltpu.SemaphoreType.DMA((planes,)),
             pltpu.SemaphoreType.DMA((2,)),
             pltpu.SemaphoreType.DMA((2,)),
-            pltpu.SemaphoreType.DMA((2,)),
+            pltpu.SemaphoreType.DMA((height // CHUNK,)),
+            pltpu.SemaphoreType.DMA((height // CHUNK,)),
             pltpu.SemaphoreType.DMA((count,)),
             pltpu.SemaphoreType.DMA((count,)),
         ],

time: 44.2 us -> 31.8 us (0.72)
  the two profiles are of different devices: /device:TPU:5 before, /device:TPU:1 now
where the time goes in v2:
time: 31.8 us; the launch traced here: 31.6 us
  Pallas kernels  29.8 us (94%)
  local copies, waits for them, and re-layouts  1.77 us (6%)
    pallas_call x1, Pallas kernels, body(): pl.pallas_call(functools.partial(kernel, count), out_shape=jax.ShapeDtype...  29.8 us
    unnamed x1, local copies, waits for them, and re-layouts  1.77 us

profile of v2, /device:TPU:1, one launch (start us, length us, event | category | flops | bytes accessed | tf_op | source)
XLA Modules:
  0.0 31.6 jit_solution(13827936153688804902)
XLA Ops:
  0.0 29.8 %encoder.1 = bf16[1,16,24,512]{3,2,1,0:T(8,128)(2,1)} custom-call(bf16[2,32,48,256]{3,2,1,0:T(8,128)(2,1)} %vol_hbm.1, f32[1,256]{1,0:T(1,128)} %bitcast.2, f32[1,256]{1,0:T(1,128)} %bitcast.3, bf16[27,256,256]{2,1,0:T(8,128)(2,1)} %conv_hbm.1, bf16[8,256,512]{2,1,0:T(8,128)(2,1)} %down_hbm.1), custom_call_target="tpu_custom_call" | custom-call | tf_op jit(solution)/shard_map/encoder/pallas_call | solution.py:257
  29.8 1.8 %copy.7 = bf16[1,16,24,512]{3,2,1,0:T(8,128)(2,1)} copy(bf16[1,16,24,512]{3,2,1,0:T(8,128)(2,1)} %encoder.1) | data formatting | bytes 786432

commit v3 on v2

--- a/solution.py
+++ b/solution.py
@@ -9,7 +9,7 @@
 
 GROUPS = 32
 LANES = 128
-ROWS = 8
+ROWS = 16
 CHUNK = 8
 NROWS = 2
 MESH = pl.DeviceIdType.MESH
@@ -43,7 +43,6 @@
     down_copy = pltpu.make_async_copy(down_hbm, down_w, w_sem.at[1])
     conv_copy.start()
     down_copy.start()
-    pl.semaphore_wait(barrier, count - 1)
 
     odd = lax.rem(me, 2)
     even = 1 - odd
@@ -92,6 +91,7 @@
         stat_copy(k).start()
         return 0
 
+    pl.semaphore_wait(barrier, count - 1)
     lax.fori_loop(1, count, send, 0)
 
     near_copy.start()
@@ -139,23 +139,23 @@
         first = first | (nrow == r * width)
         last = last | (nrow == r * width + width - 1)
 
+    def normalise_rows(source, plane, h):
+        block = source[pl.ds(h, NROWS)].astype(jnp.float32)
+        block = block.reshape(NROWS * width, chans) * scale + shift
+        before = jnp.where(first, 0.0, pltpu.roll(block, 1, 0))
+        after = jnp.where(last, 0.0, pltpu.roll(block, NROWS * width - 1, 0))
+        for c, value in enumerate((before, block, after)):
+            taps[plane, pl.ds(h + 1, NROWS), :, c * chans : (c + 1) * chans] = value.astype(
+                jnp.bfloat16
+            ).reshape(NROWS, width, chans)
+
     def normalise(source, plane, start, stop):
         def one(i, _):
-            h = i * NROWS
-            block = source[pl.ds(h, NROWS)].astype(jnp.float32)
-            block = block.reshape(NROWS * width, chans) * scale + shift
-            before = jnp.where(first, 0.0, pltpu.roll(block, 1, 0))
-            after = jnp.where(last, 0.0, pltpu.roll(block, NROWS * width - 1, 0))
-            for c, value in enumerate((before, block, after)):
-                taps[plane, pl.ds(h + 1, NROWS), :, c * chans : (c + 1) * chans] = value.astype(
-                    jnp.bfloat16
-                ).reshape(NROWS, width, chans)
+            normalise_rows(source, plane, i * NROWS)
             return 0
 
         lax.fori_loop(start // NROWS, stop // NROWS, one, 0, unroll=2)
 
-    for p in range(planes):
-        normalise(vol.at[p], p + 1, 0, height)
     conv_copy.wait()
 
     def window(plane, h, rows):
@@ -170,18 +170,27 @@
     def weight(a):
         return conv_w[pl.ds(9 * a, 9)].reshape(9 * chans, chans)
 
-    def inner(i, _):
-        h = i * ROWS
-        lhs = [window(p + 1, h, ROWS) for p in range(2)]
+    def inner(h, rows):
+        lhs = [window(p + 1, h, rows) for p in range(2)]
         for out in range(2):
             value = jnp.dot(lhs[0], weight(1 - out), preferred_element_type=jnp.float32)
             value += jnp.dot(lhs[1], weight(2 - out), preferred_element_type=jnp.float32)
-            value = value.reshape(ROWS, width, chans)
+            value = value.reshape(rows, width, chans)
             for part in range(chans // LANES):
-                acc[part, out, pl.ds(h, ROWS)] = value[:, :, part * LANES : (part + 1) * LANES]
-        return 0
-
-    lax.fori_loop(0, height // ROWS, inner, 0)
+                acc[part, out, pl.ds(h, rows)] = value[:, :, part * LANES : (part + 1) * LANES]
+
+    ahead = (8, 16, 24, height)
+    for p in range(planes):
+        normalise(vol.at[p], p + 1, 0, ahead[0])
+    done = 0
+    for k, ready in enumerate(ahead):
+        if ready < height:
+            for p in range(planes):
+                for h in range(ready, ahead[k + 1], NROWS):
+                    normalise_rows(vol.at[p], p + 1, h)
+        until = height if ready == height else ready - 1
+        inner(done, until - done)
+        done = until
 
     def finish(out, h, rows):
         value = jnp.dot(

time: 31.8 us -> 30.4 us (0.956)
  Pallas kernels: 29.8 us -> 28.2 us
    pallas_call x1, Pallas kernels: 29.8 us -> 28.2 us  [body(): pl.pallas_call(functools.partial(kernel, count), out_shape=jax.ShapeDtype...]
where the time goes in v3:
time: 30.4 us; the launch traced here: 30 us
  Pallas kernels  28.2 us (93%)
  local copies, waits for them, and re-layouts  1.77 us (6%)
    pallas_call x1, Pallas kernels, body(): pl.pallas_call(functools.partial(kernel, count), out_shape=jax.ShapeDtype...  28.2 us
    unnamed x1, local copies, waits for them, and re-layouts  1.77 us

profile of v3, /device:TPU:1, one launch (start us, length us, event | category | flops | bytes accessed | tf_op | source)
XLA Modules:
  0.0 30.0 jit_solution(3513351331590565208)
XLA Ops:
  0.0 28.2 %encoder.1 = bf16[1,16,24,512]{3,2,1,0:T(8,128)(2,1)} custom-call(bf16[2,32,48,256]{3,2,1,0:T(8,128)(2,1)} %vol_hbm.1, f32[1,256]{1,0:T(1,128)} %bitcast.2, f32[1,256]{1,0:T(1,128)} %bitcast.3, bf16[27,256,256]{2,1,0:T(8,128)(2,1)} %conv_hbm.1, bf16[8,256,512]{2,1,0:T(8,128)(2,1)} %down_hbm.1), custom_call_target="tpu_custom_call" | custom-call | tf_op jit(solution)/shard_map/encoder/pallas_call | solution.py:266
  28.2 1.8 %copy.7 = bf16[1,16,24,512]{3,2,1,0:T(8,128)(2,1)} copy(bf16[1,16,24,512]{3,2,1,0:T(8,128)(2,1)} %encoder.1) | data formatting | bytes 786432
